TPU v7x, 32 devices: a whole 2x2x4 slice. The times are simulated.
32 devices in a mesh: batch: 8 (over z, x), rep: 4 (over y, core).
Axes of the slice: x: 2, y: 2, z: 4, core: 2. Of those that a mesh axis runs over, the one named last changes fastest.
Arguments:
- latents: bfloat16 [4, 16, 512, 1024], P('rep', 'batch'), may hold values from -6 to 6
- query_key_value_weight: bfloat16 [1024, 3072], P('batch'), may hold values from -0.1875 to 0.1875
- output_weight: bfloat16 [1024, 1024], P('batch'), may hold values from -1.5 to 1.5
- up_weight: bfloat16 [1024, 1024], P('batch'), may hold values from -0.1875 to 0.1875
- down_weight: bfloat16 [1024, 1024], P('batch'), may hold values from -0.1875 to 0.1875
- norm_gains: bfloat16 [2, 1024], P(None, 'batch'), may hold values from 0.099609375 to 1.8984375
- biases: bfloat16 [6, 1024], P(None, 'batch'), may hold values from -1.5 to 1.5
- feed_forward_bias: bfloat16 [1024], P('batch'), may hold values from -1.5 to 1.5
- cotangent: bfloat16 [4, 16, 512, 1024], P('rep', 'batch'), may hold values from -6 to 6
Outputs:
- out_latents: bfloat16 [4, 16, 512, 1024], P('rep', 'batch')
- grad_latents: bfloat16 [4, 16, 512, 1024], P('rep', 'batch')
- grad_w_qkv: float32 [1024, 3072], P('batch')
- grad_w_out: float32 [1024, 1024], P('batch')
- grad_w_up: float32 [1024, 1024], P('batch')
- grad_w_down: float32 [1024, 1024], P('batch')
- grad_gains: float32 [2, 1024], P(None, 'batch')
- grad_biases: float32 [6, 1024], P(None, 'batch')
- grad_mlp_bias: float32 [1024], P('batch')
All inputs are finite; a program needn't handle non-finite values.
Results may differ from a plain program's by a relative error of at most 0.014.
The roundings to bfloat16 on the way count: a program that leaves them out, or rounds other values in their place, can miss the bound.
Values may be sent and summed in bfloat16 or wider, within the bound.
No kernel may reach another device: no remote copies, remote signals or barrier semaphores. Data moves between devices by JAX's collectives and lax.ppermute only.
A program may use at most 192 MiB of HBM per device.

v0:
```python
import jax
import jax.numpy as jnp
from jax import lax
from jax.sharding import PartitionSpec as P

HEADS = 8
EPS = 1e-05
AXES = ("batch", "rep")
BF = jnp.bfloat16
F32 = jnp.float32


def layer_norm(values, gain, shift):
    mean = jnp.mean(values, axis=-1, keepdims=True)
    centred = values - mean
    spread = jnp.mean(centred * centred, axis=-1, keepdims=True)
    return centred * lax.rsqrt(spread + EPS) * gain + shift


def permutation(move, nb, nr):
    pairs = []
    for b in range(nb):
        for r in range(nr):
            tb, tr = move(b, r)
            pairs.append((b * nr + r, tb * nr + tr))
    return pairs


class Links:

    def __init__(self, nb, nr):

        def swap(kb, kr):
            return permutation(lambda b, r: (b ^ kb, r ^ kr), nb, nr)

        self.core = swap(0, 1)
        self.rep = [swap(0, 1), swap(0, 2), swap(0, 3)]
        self.z = [swap(2, 0), swap(4, 0), swap(6, 0)]
        self.y_or_x = permutation(lambda b, r: (b, r ^ 2) if r % 2 == 0 else (b ^ 1, r), nb, nr)
        self.x_or_y = permutation(lambda b, r: (b ^ 1, r) if r % 2 == 0 else (b, r ^ 2), nb, nr)
        batch, rep = (lax.axis_index("batch"), lax.axis_index("rep"))
        self.xi, self.zi = (batch % 2, batch // 2)
        self.ci, self.yi = (rep % 2, rep // 2)


def move(value, pairs):
    return lax.ppermute(value, AXES, pairs)


def flip_if(bit, value, axis):
    return jnp.where(bit == 1, jnp.flip(value, axis), value)


def gather_rows(local, links):
    rows, n = local.shape
    quarter = lax.dynamic_index_in_dim(
        local.reshape(4, rows // 4, n), links.ci * 2 + links.yi, 0, keepdims=False
    )
    own = jnp.stack([quarter] + [move(quarter, p) for p in links.z])
    first = move(own, links.y_or_x)
    second = move(own, links.x_or_y)
    third = move(first, links.x_or_y)
    halves = []
    here = [own, first, second, third]
    there = [move(part, links.core) for part in here]
    for parts, core in ((here, links.ci), (there, 1 - links.ci)):
        a, f, s, t = parts
        dx = jnp.where(core == 1, f, s)
        dy = jnp.where(core == 1, s, f)
        halves.append(jnp.stack([jnp.stack([a, dy]), jnp.stack([dx, t])]))
    whole = jnp.stack(halves)
    whole = flip_if(links.ci, whole, 0)
    whole = flip_if(links.xi, whole, 1)
    whole = flip_if(links.yi, whole, 2)
    whole = flip_if(links.zi % 2, whole.reshape(2, 2, 2, 2, 2, rows // 4, n), 4)
    whole = flip_if(links.zi // 2, whole, 3)
    whole = whole.transpose(3, 4, 1, 0, 2, 5, 6)
    return whole.reshape(8 * rows, n)


def reduce_rows(partial, links):
    total, n = partial.shape
    rows, q = (total // 8, n // 4)
    view = partial.reshape(4, 2, rows, 2, 2, q)
    view = view.transpose(3, 1, 4, 0, 2, 5)
    keep = lax.dynamic_index_in_dim(view, links.ci, 0, keepdims=False)
    send = lax.dynamic_index_in_dim(view, 1 - links.ci, 0, keepdims=False).astype(BF)
    held = keep + move(send, links.core).astype(F32)
    held = jnp.where(links.ci == 0, held, held.transpose(1, 0, 2, 3, 4))
    mine = jnp.where(links.ci == 0, links.xi, links.yi)
    keep = lax.dynamic_index_in_dim(held, mine, 0, keepdims=False)
    send = lax.dynamic_index_in_dim(held, 1 - mine, 0, keepdims=False).astype(BF)
    held = keep + move(send, links.x_or_y).astype(F32)
    mine = jnp.where(links.ci == 0, links.yi, links.xi)
    keep = lax.dynamic_index_in_dim(held, mine, 0, keepdims=False)
    send = lax.dynamic_index_in_dim(held, 1 - mine, 0, keepdims=False).astype(BF)
    held = keep + move(send, links.y_or_x).astype(F32)
    out = lax.dynamic_index_in_dim(held, links.zi, 0, keepdims=False)
    for k, pairs in enumerate(links.z):
        send = lax.dynamic_index_in_dim(held, links.zi ^ k + 1, 0, keepdims=False).astype(BF)
        out = out + move(send, pairs).astype(F32)
    out = out.astype(BF)
    by_core, by_y, by_both = [move(out, p) for p in links.rep]
    grid = jnp.stack([jnp.stack([out, by_y]), jnp.stack([by_core, by_both])])
    grid = flip_if(links.yi, flip_if(links.ci, grid, 0), 1)
    return grid.transpose(2, 0, 1, 3).reshape(rows, n).astype(F32)


def heads_of(packed):
    images, length, width = packed.shape
    size = width // 3 // HEADS
    view = packed.reshape(images, length, 3, HEADS, size)
    return (view[:, :, 0], view[:, :, 1], view[:, :, 2], size ** (-0.5))


def per_device(latents, w_qkv, w_out, w_up, w_down, gains, biases, ff_bias, cotangent, *, nb, nr):
    reps, images, length, width = latents.shape
    x = latents.reshape(-1, width).astype(F32)
    cot = cotangent.reshape(-1, width)
    count = reps * images
    small = jnp.concatenate([gains, biases, ff_bias[None]], axis=0)
    native = nb != 8 or nr != 4
    if native:
        small = lax.all_gather(small, "batch", axis=1, tiled=True)
        w_qkv, w_out, w_up, w_down = (
            lax.all_gather(w, "batch", axis=0, tiled=True) for w in (w_qkv, w_out, w_up, w_down)
        )
    else:
        links = Links(nb, nr)
        small = lax.all_gather(small, "batch", axis=1, tiled=True)
        w_qkv = gather_rows(w_qkv, links)
        rest = gather_rows(jnp.concatenate([w_out, w_up, w_down], axis=1), links)
        w_out, w_up, w_down = (rest[:, :width], rest[:, width:-width], rest[:, -width:])
    small = small.astype(F32)
    g1, g2 = (small[0], small[1])
    b1, bq, bv, bo, b2, bd, bu = (small[i] for i in range(2, 9))

    def dot(a, b, dims):
        return lax.dot_general(a, b, (dims, ((), ())), preferred_element_type=F32)

    NN, NT, TN = (((1,), (0,)), ((1,), (1,)), ((0,), (0,)))
    first, pull_one = jax.vjp(layer_norm, x, g1, b1)
    first = first.astype(BF)
    packed = dot(first, w_qkv, NN) + jnp.concatenate([bq, jnp.zeros_like(bq), bv])
    packed = packed.astype(BF).reshape(count, length, 3 * width)
    q, k, v, scale = heads_of(packed)
    scores = jnp.einsum("iqhd,ikhd->ihqk", q, k, preferred_element_type=F32) * scale
    top = jnp.max(scores, axis=-1, keepdims=True)
    raised = jnp.exp(scores - top)
    p = raised / jnp.sum(raised, axis=-1, keepdims=True)
    probs = p.astype(BF)
    mixed = jnp.einsum("ihqk,ikhd->iqhd", probs, v, preferred_element_type=F32)
    mixed = mixed.astype(BF).reshape(-1, width)
    middle = x + dot(mixed, w_out, NN) + bo
    second, pull_two = jax.vjp(layer_norm, middle, g2, b2)
    second = second.astype(BF)
    hidden = dot(second, w_up, NN) + bu
    active, pull_gelu = jax.vjp(jax.nn.gelu, hidden)
    active = active.astype(BF)
    out = (middle + dot(active, w_down, NN) + bd).astype(BF)
    gw_down = dot(active, cot, TN)
    gb_down = jnp.sum(cot.astype(F32), axis=0)
    g_hidden = pull_gelu(dot(cot, w_down, NT))[0].astype(BF)
    gw_up = dot(second, g_hidden, TN)
    gb_up = jnp.sum(g_hidden.astype(F32), axis=0)
    g_mid, gg2, gb2 = pull_two(dot(g_hidden, w_up, NT))
    g_middle = cot.astype(F32) + g_mid
    g_attn = g_middle.astype(BF)
    gw_out = dot(mixed, g_attn, TN)
    gb_out = jnp.sum(g_attn.astype(F32), axis=0)
    g_mixed = dot(g_attn, w_out, NT).astype(BF).reshape(count, length, HEADS, -1)
    g_v = jnp.einsum("ihqk,iqhd->ikhd", probs, g_mixed, preferred_element_type=F32)
    g_p = jnp.einsum("iqhd,ikhd->ihqk", g_mixed, v, preferred_element_type=F32)
    g_s = (p * (g_p - jnp.sum(g_p * p, axis=-1, keepdims=True))).astype(BF)
    g_q = jnp.einsum("ihqk,ikhd->iqhd", g_s, k, preferred_element_type=F32) * scale
    g_k = jnp.einsum("ihqk,iqhd->ikhd", g_s, q, preferred_element_type=F32) * scale
    g_packed = jnp.stack([g_q, g_k, g_v], axis=2).astype(BF).reshape(-1, 3 * width)
    gw_qkv = dot(first, g_packed, TN)
    gb_packed = jnp.sum(g_packed.astype(F32), axis=0)
    g_in, gg1, gb1 = pull_one(dot(g_packed, w_qkv, NT))
    g_lat = (g_middle + g_in).astype(BF)
    zero = jnp.zeros_like(gb_up)
    smalls = jnp.stack(
        [gg1, gg2, gb1, gb_packed[:width], gb_packed[2 * width :], gb_out, gb2, gb_down, gb_up]
        + [zero] * 7
    )
    smalls = lax.psum(smalls, AXES)
    smalls = lax.dynamic_slice_in_dim(
        smalls, lax.axis_index("batch") * (width // nb), width // nb, 1
    )
    if native:

        def reduced(g):
            g = lax.psum_scatter(g, "batch", scatter_dimension=0, tiled=True)
            return lax.psum(g.astype(BF), "rep").astype(F32)

        gw_qkv, gw_out, gw_up, gw_down = (reduced(g) for g in (gw_qkv, gw_out, gw_up, gw_down))
    else:
        rest = reduce_rows(jnp.concatenate([gw_out, gw_up, gw_down], axis=1), links)
        gw_qkv = reduce_rows(gw_qkv, links)
        gw_out, gw_up, gw_down = (rest[:, :width], rest[:, width:-width], rest[:, -width:])
    return (
        out.reshape(latents.shape),
        g_lat.reshape(latents.shape),
        gw_qkv,
        gw_out,
        gw_up,
        gw_down,
        smalls[:2],
        smalls[2:8],
        smalls[8],
    )


def solution(mesh):
    nb, nr = (mesh.shape["batch"], mesh.shape["rep"])

    def body(*args):
        return per_device(*args, nb=nb, nr=nr)

    rows = P("batch", None)
    cols = P(None, "batch")
    data = P("rep", "batch", None, None)
    return jax.shard_map(
        body,
        mesh=mesh,
        in_specs=(data, rows, rows, rows, rows, cols, cols, P("batch"), data),
        out_specs=(data, data, rows, rows, rows, rows, cols, cols, P("batch")),
        check_vma=False,
    )
```

profile of v0, /device:TPU:0, one launch (start us, length us, event | category | flops | bytes accessed | tf_op | source)
XLA Modules:
  0.0 650.0 jit_solution(16085910962180508302)
XLA Ops:
  20.9 45.8 %all_gather.3 = bf16[9,1024]{1,0:T(8,128)(2,1)S(1)} all-gather(bf16[9,128]{1,0:T(8,128)(2,1)S(1)} %pad_maximum_fusion.9), channel_id=1, replica_groups=mesh['batch'=8,'rep'=4] {'batch'}, dimensions={1}, use_global_device_ids=true | all-gather | bytes 20736 | tf_op jit(solution)/shard_map/all_gather | solution.py:130
  77.2 7.4 %collective-permute-done.4 = bf16[4,32,3072]{2,1,0:T(8,128)(2,1)} collective-permute-done((bf16[4,32,3072]{2,1,0:T(8,128)(2,1)}, bf16[4,32,3072]{2,1,0:T(8,128)(2,1)}, u32[]{:S(2)}, u32[]{:S(2)}) %collective-permute-start.4) | collective-permute-done | bytes 786464 | tf_op jit(solution)/shard_map/ppermute | solution.py:47
  89.4 12.0 %collective-permute-done.14 = bf16[4,32,3072]{2,1,0:T(8,128)(2,1)S(1)} collective-permute-done((bf16[4,32,3072]{2,1,0:T(8,128)(2,1)S(1)}, bf16[4,32,3072]{2,1,0:T(8,128)(2,1)S(1)}, u32[]{:S(2)}, u32[]{:S(2)}) %collective-permute-start.14) | collective-permute-done | bytes 786464 | tf_op jit(solution)/shard_map/ppermute | solution.py:47
  107.8 8.4 %collective-permute-done.15 = bf16[4,32,3072]{2,1,0:T(8,128)(2,1)} collective-permute-done((bf16[4,32,3072]{2,1,0:T(8,128)(2,1)S(1)}, bf16[4,32,3072]{2,1,0:T(8,128)(2,1)}, u32[]{:S(2)}, u32[]{:S(2)}) %collective-permute-start.15) | collective-permute-done | bytes 786464 | tf_op jit(solution)/shard_map/ppermute | solution.py:47
  130.7 7.5 %reverse_select_fusion.4 = bf16[2,2,2,4,32,3072]{5,4,3,2,1,0:T(8,128)(2,1)S(1)} fusion(bf16[2,2,2,4,32,3072]{5,4,3,2,1,0:T(8,128)(2,1)} %pad_maximum_fusion.2, pred[]{:T(512)S(6)} %eq.23), kind=kLoop, calls=%fused_computation.14 | loop fusion | flops 3145728 | bytes 12582913 | tf_op jit(solution)/shard_map/jit(_where)/select_n | solution.py:51
  147.0 7.6 %reverse_select_fusion.7 = bf16[2,2,2,4,32,3072]{5,4,2,0,1,3:T(8,128)(2,1)S(1)} fusion(bf16[2,2,2,4,32,3072]{5,4,2,0,1,3:T(8,128)(2,1)} %reverse_select_fusion.8, pred[]{:T(512)S(6)} %eq.21), kind=kLoop, calls=%fused_computation.17 | loop fusion | flops 3145728 | bytes 12582913 | tf_op jit(solution)/shard_map/jit(_where)/select_n | solution.py:51
  169.0 7.5 %reverse_select_fusion.5 = bf16[2,2,2,2,2,32,3072]{6,5,2,0,1,4,3:T(8,128)(2,1)S(1)} fusion(bf16[2,2,2,2,2,32,3072]{6,5,2,0,1,4,3:T(8,128)(2,1)} %reverse_select_fusion.6, pred[]{:T(512)S(6)} %eq.19), kind=kLoop, calls=%fused_computation.15 | loop fusion | flops 3145728 | bytes 12582913 | tf_op jit(solution)/shard_map/jit(_where)/select_n | solution.py:51
  181.3 8.6 %fusion.5 = bf16[128,8,24,128]{3,1,2,0:T(8,128)(2,1)} fusion(f32[3072]{0:T(1024)S(1)} %pad_maximum_fusion.8, bf16[1024,1024]{1,0:T(8,128)(2,1)S(1)} %bitcast.349, bf16[1024,3072]{1,0:T(8,128)(2,1)S(1)} %bitcast.343), kind=kOutput, calls=%fused_computation.22 | convolution fusion | flops 6448742400 | bytes 14692352 | tf_op jit(solution)/shard_map/dot_general | solution.py:139
  202.3 10.4 %fusion.52 = f32[2,8,512,512]{2,3,1,0:T(8,128)} fusion(bf16[2,512,1,8,128]{4,3,2,1,0:T(8,128)(2,1)} %get-tuple-element.33, bf16[2,512,1,8,128]{4,3,2,1,0:T(8,128)(2,1)} %get-tuple-element.31), kind=kOutput, calls=%fused_computation.106 | convolution fusion | flops 1073741824 | bytes 20971520 | tf_op jit(solution)/shard_map/iqhd,ikhd->ihqk/dot_general | solution.py:147
  212.6 18.9 %fusion.100 = (f32[2,8,512]{2,1,0:T(8,128)S(1)}, f32[2,8,512,512]{2,3,1,0:T(8,128)}) fusion(f32[2,8,512,512]{2,3,1,0:T(8,128)} %fusion.52), kind=kOutput, calls=%fused_computation.208 | output fusion | flops 16777728 | bytes 33587200 | tf_op jit(solution)/shard_map/sub | solution.py:149
  231.6 8.4 %convert_bitcast_fusion.2 = bf16[2,512,8,128]{1,3,2,0:T(8,128)(2,1)} fusion(bf16[2,512,1,8,128]{1,4,3,0,2:T(8,128)(2,1)S(1)} %copy-done.22, f32[2,8,512,512]{2,3,1,0:T(8,128)} %get-tuple-element.74, f32[2,8,512]{2,1,0:T(8,128)S(1)} %get-tuple-element.73), kind=kOutput, calls=%fused_computation.105 | convolution fusion | flops 1083179008 | bytes 21004288 | tf_op jit(solution)/shard_map/ihqk,ikhd->iqhd/dot_general | solution.py:152
  252.3 5.9 convert_reduce_fusion.2
  287.8 10.7 %fusion.38 = bf16[2,512,1,8,128]{1,4,3,0,2:T(8,128)(2,1)} fusion(bf16[2,512,8,128]{1,3,2,0:T(8,128)(2,1)} %copy.53, f32[2,8,512,512]{2,3,1,0:T(8,128)} %get-tuple-element.74, f32[2,8,512]{2,1,0:T(8,128)S(1)} %get-tuple-element.73), kind=kOutput, calls=%fused_computation.94 | convolution fusion | flops 1082130432 | bytes 21004288 | tf_op jit(solution)/shard_map/ihqk,iqhd->ikhd/dot_general | solution.py:172
  298.5 10.9 %multiply_reduce_fusion = (f32[2,8,512]{2,1,0:T(8,128)S(1)}, f32[2,8,512,512]{2,3,1,0:T(8,128)}) fusion(f32[2,8,512,512]{2,3,1,0:T(8,128)} %get-tuple-element.74, f32[2,8,512]{2,1,0:T(8,128)S(1)} %get-tuple-element.73, bf16[2,512,8,128]{1,3,2,0:T(8,128)(2,1)S(1)} %copy-done.25, bf16[2,512,1,8,128]{1,4,3,0,2:T(8,128)(2,1)S(1)} %copy-done.23), kind=kOutput, calls=%fused_computation.2 | convolution fusion | flops 1086316544 | bytes 37814272 | tf_op jit(solution)/shard_map/iqhd,ikhd->ihqk/dot_general | solution.py:173
  309.4 11.9 %multiply_convert_fusion = bf16[2,8,512,512]{2,3,1,0:T(8,128)(2,1)S(1)} fusion(f32[2,8,512,512]{2,3,1,0:T(8,128)} %get-tuple-element.79, f32[2,8,512]{2,1,0:T(8,128)S(1)} %get-tuple-element.78, f32[2,8,512,512]{2,3,1,0:T(8,128)} %get-tuple-element.74, f32[2,8,512]{2,1,0:T(8,128)S(1)} %get-tuple-element.73), kind=kLoop, calls=%fused_computation.1 | loop fusion | flops 16777216 | bytes 42008576 | tf_op jit(solution)/shard_map/convert_element_type | solution.py:174
  330.9 5.7 pad_maximum_fusion
  336.7 16.9 %reshape.232 = f32[4,2,128,2,2,768]{2,1,0,5,4,3:T(2,128)} reshape(f32[1024,3072]{0,1:T(8,128)} %pad_maximum_fusion) | data formatting | bytes 25165824 | tf_op jit(solution)/shard_map/reshape | solution.py:84
  353.6 6.6 %constant_dynamic-slice_fusion.1 = bf16[4,2,128,1,2,768]{2,1,0,5,4,3:T(2,128)(2,1)} fusion(f32[4,2,128,2,2,768]{2,1,0,5,4,3:T(2,128)} %reshape.232, s32[]{:T(128)S(6)} %select_n.250), kind=kLoop, calls=%fused_computation.178 | loop fusion | bytes 6291460 | tf_op jit(solution)/shard_map/jit(dynamic_index_in_dim)/dynamic_slice | solution.py:87
  360.1 8.7 %copy.89 = bf16[4,2,128,1,2,768]{5,2,0,1,4,3:T(8,128)(2,1)} copy(bf16[4,2,128,1,2,768]{2,1,0,5,4,3:T(2,128)(2,1)} %constant_dynamic-slice_fusion.1) | data formatting | bytes 6291456
  369.2 6.1 convert_reduce_fusion
  375.3 9.2 %copy.55 = bf16[2,512,3,8,128]{4,3,2,1,0:T(8,128)(2,1)} copy(bf16[2,512,3,8,128]{1,4,3,0,2:T(8,128)(2,1)} %get-tuple-element.28) | data formatting | bytes 12582912 | tf_op jit(solution)/shard_map/convert_element_type | solution.py:177
  384.5 10.3 %convert_element_type.247 = bf16[1024,3072]{1,0:T(8,128)(2,1)} reshape(bf16[2,512,3,8,128]{4,3,2,1,0:T(8,128)(2,1)} %copy.55) | data formatting | bytes 12582912 | tf_op jit(solution)/shard_map/convert_element_type | solution.py:177
  394.8 12.4 %fusion.93 = (f32[1024]{0:T(1024)S(1)}, f32[1024]{0:T(1024)S(1)}, f32[1024,1024]{1,0:T(8,128)}) fusion(f32[1024]{0:T(1024)S(1)} %bitcast.371, f32[1024]{0:T(1024)S(1)} %bitcast.376, bf16[1,2,512,1024]{3,2,1,0:T(8,128)(2,1)S(1)} %copy-done.2, bf16[1024,3072]{1,0:T(8,128)(2,1)} %convert_element_type.247, bf16[1024,3072]{1,0:T(8,128)(2,1)} %bitcast.344), kind=kOutput, calls=%fused_computation.202 | convolution fusion | flops 6448740352 | bytes 18890752 | tf_op jit(solution)/shard_map/dot_general | solution.py:139
  407.2 8.9 %copy.56 = bf16[3072,1024]{1,0:T(8,128)(2,1)} copy(bf16[3072,1024]{0,1:T(8,128)(2,1)} %bitcast.325) | data formatting | bytes 12582912 | tf_op jit(solution)/shard_map/dot_general | solution.py:139
  425.2 9.5 %fusion.102 = f32[4,2,128,2,2,768]{5,2,4,3,1,0:T(8,128)S(1)} fusion(bf16[4,2,128,1024,1,1]{3,2,5,4,1,0:T(8,128)(2,1)} %bitcast.352, bf16[2,2,768,1024,1,1]{3,2,1,0,5,4:T(8,128)(2,1)} %bitcast.345), kind=kOutput, calls=%fused_computation.210 | convolution fusion | flops 6442450944 | bytes 20971520 | tf_op jit(solution)/shard_map/dot_general | solution.py:139
  443.4 7.6 %constant_dynamic-slice_fusion.2 = f32[4,2,128,1,2,768]{2,1,0,5,4,3:T(2,128)} fusion(f32[4,2,128,2,2,768]{2,1,0,5,4,3:T(2,128)} %reshape.232, s32[]{:T(128)S(6)} %select_n.249), kind=kLoop, calls=%fused_computation.179 | loop fusion | bytes 12582916 | tf_op jit(solution)/shard_map/dynamic-slice.2
  451.0 10.5 %copy.88 = f32[4,2,128,1,2,768]{5,2,0,1,4,3:T(8,128)} copy(f32[4,2,128,1,2,768]{2,1,0,5,4,3:T(2,128)} %constant_dynamic-slice_fusion.2) | data formatting | bytes 12582912
  480.5 8.5 %add_convert_fusion.2 = bf16[1024,1024]{1,0:T(8,128)(2,1)} fusion(f32[1024,1024]{1,0:T(8,128)} %copy-done.10, f32[1024]{0:T(1024)S(1)} %bitcast.394, bf16[1024,3072]{1,0:T(8,128)(2,1)} %bitcast.336, f32[1024,1024]{1,0:T(8,128)} %copy-done.42, f32[1024]{0:T(1024)S(1)} %bitcast.393), kind=kOutput, calls=%fused_computation.75 | convolution fusion | flops 2161115136 | bytes 12591104 | tf_op jit(solution)/shard_map/dot_general | solution.py:139
  491.5 22.9 %collective-permute-done.21 = bf16[2,4,128,768]{3,2,0,1:T(8,128)(2,1)S(1)} collective-permute-done((bf16[2,4,128,768]{3,2,0,1:T(8,128)(2,1)S(1)}, bf16[2,4,128,768]{3,2,0,1:T(8,128)(2,1)S(1)}, u32[]{:S(2)}, u32[]{:S(2)}) %collective-permute-start.21) | collective-permute-done | bytes 1572896 | tf_op jit(solution)/shard_map/ppermute | solution.py:47
  520.9 58.8 %all-reduce.2.cloned.1.call-done = f32[16,1024]{1,0:T(8,128)} async-done(((f32[16,1024]{1,0:T(8,128)}), f32[16,1024]{1,0:T(8,128)}) %all-reduce.2.cloned.1.call-update) | async-done | bytes 65552 | tf_op jit(solution)/shard_map/psum | solution.py:187
  600.3 16.3 %collective-permute-done.33 = bf16[128,768]{1,0:T(8,128)(2,1)S(1)} collective-permute-done((bf16[128,768]{1,0:T(8,128)(2,1)S(1)}, bf16[128,768]{1,0:T(8,128)(2,1)S(1)}, u32[]{:S(2)}, u32[]{:S(2)}) %collective-permute-start.33) | collective-permute-done | bytes 196640 | tf_op jit(solution)/shard_map/ppermute | solution.py:47
  618.9 5.7 collective-permute-done.24
  (279 shorter events, 228.1 us)
Async XLA Ops:
  7.2 572.5 %all-reduce.2.cloned.1.call-start = ((), (), s32[]{:S(2)}) async-start(), calls=%async_computation | async-start | bytes 131072 | tf_op jit(solution)/shard_map/psum | solution.py:187
  8.3 59.0 %collective-permute-start.2 = (bf16[32,3072]{1,0:T(8,128)(2,1)S(1)}, bf16[32,3072]{1,0:T(8,128)(2,1)S(1)}, u32[]{:S(2)}, u32[]{:S(2)}) collective-permute-start(bf16[32,3072]{1,0:T(8,128)(2,1)S(1)} %fusion.119), channel_id=1, source_target_pairs={{0,24},{1,25},{2,26},{3,27},{4,28},{5,29},{6,30},{7,31},{8,16},{9,... | collective-permute-start | bytes 589832 | tf_op jit(solution)/shard_map/ppermute | solution.py:47
  13.4 54.2 %collective-permute-start.1 = (bf16[32,3072]{1,0:T(8,128)(2,1)S(1)}, bf16[32,3072]{1,0:T(8,128)(2,1)S(1)}, u32[]{:S(2)}, u32[]{:S(2)}) collective-permute-start(bf16[32,3072]{1,0:T(8,128)(2,1)S(1)} %fusion.119), channel_id=1, source_target_pairs={{0,16},{1,17},{2,18},{3,19},{4,20},{5,21},{6,22},{7,23},{8,24},{9,... | collective-permute-start | bytes 589832 | tf_op jit(solution)/shard_map/ppermute | solution.py:47
  13.5 54.2 %collective-permute-start = (bf16[32,3072]{1,0:T(8,128)(2,1)S(1)}, bf16[32,3072]{1,0:T(8,128)(2,1)S(1)}, u32[]{:S(2)}, u32[]{:S(2)}) collective-permute-start(bf16[32,3072]{1,0:T(8,128)(2,1)S(1)} %fusion.119), channel_id=1, source_target_pairs={{0,8},{1,9},{2,10},{3,11},{4,12},{5,13},{6,14},{7,15},{8,0},{9,1},... | collective-permute-start | bytes 589832 | tf_op jit(solution)/shard_map/ppermute | solution.py:47
  16.0 57.5 %collective-permute-start.12 = (bf16[32,3072]{1,0:T(8,128)(2,1)}, bf16[32,3072]{1,0:T(8,128)(2,1)S(1)}, u32[]{:S(2)}, u32[]{:S(2)}) collective-permute-start(bf16[32,3072]{1,0:T(8,128)(2,1)} %fusion.120), channel_id=1, source_target_pairs={{0,24},{1,25},{2,26},{3,27},{4,28},{5,29},{6,30},{7,31},{8,16},{9,... | collective-permute-start | bytes 589832 | tf_op jit(solution)/shard_map/ppermute | solution.py:47
  19.7 53.9 %collective-permute-start.11 = (bf16[32,3072]{1,0:T(8,128)(2,1)}, bf16[32,3072]{1,0:T(8,128)(2,1)S(1)}, u32[]{:S(2)}, u32[]{:S(2)}) collective-permute-start(bf16[32,3072]{1,0:T(8,128)(2,1)} %fusion.120), channel_id=1, source_target_pairs={{0,16},{1,17},{2,18},{3,19},{4,20},{5,21},{6,22},{7,23},{8,24},{9,... | collective-permute-start | bytes 589832 | tf_op jit(solution)/shard_map/ppermute | solution.py:47
  68.6 16.0 %collective-permute-start.4 = (bf16[4,32,3072]{2,1,0:T(8,128)(2,1)}, bf16[4,32,3072]{2,1,0:T(8,128)(2,1)}, u32[]{:S(2)}, u32[]{:S(2)}) collective-permute-start(bf16[4,32,3072]{2,1,0:T(8,128)(2,1)} %get-tuple-element.53), channel_id=1, source_target_pairs={{0,2},{1,5},{2,0},{3,7},{4,6},{5,1},{6,4},{7,3},{8,10},{9,13},{10,... | collective-permute-start | bytes 2359304 | tf_op jit(solution)/shard_map/ppermute | solution.py:47
  70.1 17.6 %collective-permute-start.3 = (bf16[4,32,3072]{2,1,0:T(8,128)(2,1)}, bf16[4,32,3072]{2,1,0:T(8,128)(2,1)}, u32[]{:S(2)}, u32[]{:S(2)}) collective-permute-start(bf16[4,32,3072]{2,1,0:T(8,128)(2,1)} %get-tuple-element.53), channel_id=1, source_target_pairs={{0,4},{1,3},{2,6},{3,1},{4,0},{5,7},{6,2},{7,5},{8,12},{9,11},{10,... | collective-permute-start | bytes 2359304 | tf_op jit(solution)/shard_map/ppermute | solution.py:47
  73.5 48.8 %collective-permute-start.6 = (bf16[4,32,3072]{2,1,0:T(8,128)(2,1)}, bf16[4,32,3072]{2,1,0:T(8,128)(2,1)S(1)}, u32[]{:S(2)}, u32[]{:S(2)}) collective-permute-start(bf16[4,32,3072]{2,1,0:T(8,128)(2,1)} %get-tuple-element.53), channel_id=1, source_target_pairs={{0,1},{1,0},{2,3},{3,2},{4,5},{5,4},{6,7},{7,6},{8,9},{9,8},{10,11... | collective-permute-start | bytes 2359304 | tf_op jit(solution)/shard_map/ppermute | solution.py:47
  74.7 26.7 %collective-permute-start.14 = (bf16[4,32,3072]{2,1,0:T(8,128)(2,1)S(1)}, bf16[4,32,3072]{2,1,0:T(8,128)(2,1)S(1)}, u32[]{:S(2)}, u32[]{:S(2)}) collective-permute-start(bf16[4,32,3072]{2,1,0:T(8,128)(2,1)S(1)} %get-tuple-element.55), channel_id=1, source_target_pairs={{0,2},{1,5},{2,0},{3,7},{4,6},{5,1},{6,4},{7,3},{8,10},{9,13},{10,... | collective-permute-start | bytes 2359304 | tf_op jit(solution)/shard_map/ppermute | solution.py:47
  76.0 25.4 %collective-permute-start.13 = (bf16[4,32,3072]{2,1,0:T(8,128)(2,1)S(1)}, bf16[4,32,3072]{2,1,0:T(8,128)(2,1)S(1)}, u32[]{:S(2)}, u32[]{:S(2)}) collective-permute-start(bf16[4,32,3072]{2,1,0:T(8,128)(2,1)S(1)} %get-tuple-element.55), channel_id=1, source_target_pairs={{0,4},{1,3},{2,6},{3,1},{4,0},{5,7},{6,2},{7,5},{8,12},{9,11},{10,... | collective-permute-start | bytes 2359304 | tf_op jit(solution)/shard_map/ppermute | solution.py:47
  84.6 23.0 %collective-permute-start.5 = (bf16[4,32,3072]{2,1,0:T(8,128)(2,1)}, bf16[4,32,3072]{2,1,0:T(8,128)(2,1)S(1)}, u32[]{:S(2)}, u32[]{:S(2)}) collective-permute-start(bf16[4,32,3072]{2,1,0:T(8,128)(2,1)} %collective-permute-done.4), channel_id=1, source_target_pairs={{0,4},{1,3},{2,6},{3,1},{4,0},{5,7},{6,2},{7,5},{8,12},{9,11},{10,... | collective-permute-start | bytes 2359304 | tf_op jit(solution)/shard_map/ppermute | solution.py:47
  87.7 29.7 %collective-permute-start.8 = (bf16[4,32,3072]{2,1,0:T(8,128)(2,1)}, bf16[4,32,3072]{2,1,0:T(8,128)(2,1)S(1)}, u32[]{:S(2)}, u32[]{:S(2)}) collective-permute-start(bf16[4,32,3072]{2,1,0:T(8,128)(2,1)} %collective-permute-done.4), channel_id=1, source_target_pairs={{0,1},{1,0},{2,3},{3,2},{4,5},{5,4},{6,7},{7,6},{8,9},{9,8},{10,11... | collective-permute-start | bytes 2359304 | tf_op jit(solution)/shard_map/ppermute | solution.py:47
  101.4 16.6 %collective-permute-start.7 = (bf16[4,32,3072]{2,1,0:T(8,128)(2,1)}, bf16[4,32,3072]{2,1,0:T(8,128)(2,1)S(1)}, u32[]{:S(2)}, u32[]{:S(2)}) collective-permute-start(bf16[4,32,3072]{2,1,0:T(8,128)(2,1)} %collective-permute-done.3), channel_id=1, source_target_pairs={{0,1},{1,0},{2,3},{3,2},{4,5},{5,4},{6,7},{7,6},{8,9},{9,8},{10,11... | collective-permute-start | bytes 2359304 | tf_op jit(solution)/shard_map/ppermute | solution.py:47
  101.4 14.8 %collective-permute-start.15 = (bf16[4,32,3072]{2,1,0:T(8,128)(2,1)S(1)}, bf16[4,32,3072]{2,1,0:T(8,128)(2,1)}, u32[]{:S(2)}, u32[]{:S(2)}) collective-permute-start(bf16[4,32,3072]{2,1,0:T(8,128)(2,1)S(1)} %collective-permute-done.14), channel_id=1, source_target_pairs={{0,4},{1,3},{2,6},{3,1},{4,0},{5,7},{6,2},{7,5},{8,12},{9,11},{10,... | collective-permute-start | bytes 2359304 | tf_op jit(solution)/shard_map/ppermute | solution.py:47
  107.6 10.6 %collective-permute-start.18 = (bf16[4,32,3072]{2,1,0:T(8,128)(2,1)S(1)}, bf16[4,32,3072]{2,1,0:T(8,128)(2,1)S(1)}, u32[]{:S(2)}, u32[]{:S(2)}) collective-permute-start(bf16[4,32,3072]{2,1,0:T(8,128)(2,1)S(1)} %collective-permute-done.14), channel_id=1, source_target_pairs={{0,1},{1,0},{2,3},{3,2},{4,5},{5,4},{6,7},{7,6},{8,9},{9,8},{10,11... | collective-permute-start | bytes 2359304 | tf_op jit(solution)/shard_map/ppermute | solution.py:47
  368.8 94.1 %collective-permute-start.29 = (bf16[2,2,4,128,768]{4,3,2,0,1:T(8,128)(2,1)}, bf16[2,2,4,128,768]{4,3,2,0,1:T(8,128)(2,1)}, u32[]{:S(2)}, u32[]{:S(2)}) collective-permute-start(bf16[2,2,4,128,768]{4,3,2,0,1:T(8,128)(2,1)} %bitcast.348), channel_id=1, source_target_pairs={{0,1},{1,0},{2,3},{3,2},{4,5},{5,4},{6,7},{7,6},{8,9},{9,8},{10,11... | collective-permute-start | bytes 9437192 | tf_op jit(solution)/shard_map/ppermute | solution.py:47
  441.3 28.1 %collective-permute-start.20 = (bf16[2,2,4,128,768]{4,3,1,0,2:T(8,128)(2,1)}, bf16[2,2,4,128,768]{4,3,1,0,2:T(8,128)(2,1)}, u32[]{:S(2)}, u32[]{:S(2)}) collective-permute-start(bf16[2,2,4,128,768]{4,3,1,0,2:T(8,128)(2,1)} %fusion.36), channel_id=1, source_target_pairs={{0,1},{1,0},{2,3},{3,2},{4,5},{5,4},{6,7},{7,6},{8,9},{9,8},{10,11... | collective-permute-start | bytes 9437192 | tf_op jit(solution)/shard_map/ppermute | solution.py:47
  468.2 20.8 %collective-permute-start.30 = (bf16[2,4,128,768]{3,2,1,0:T(8,128)(2,1)S(1)}, bf16[2,4,128,768]{3,2,1,0:T(8,128)(2,1)S(1)}, u32[]{:S(2)}, u32[]{:S(2)}) collective-permute-start(bf16[2,4,128,768]{3,2,1,0:T(8,128)(2,1)S(1)} %fusion.68), channel_id=1, source_target_pairs={{0,4},{1,3},{2,6},{3,1},{4,0},{5,7},{6,2},{7,5},{8,12},{9,11},{10,... | collective-permute-start | bytes 4718600 | tf_op jit(solution)/shard_map/ppermute | solution.py:47
  479.5 34.9 %collective-permute-start.21 = (bf16[2,4,128,768]{3,2,0,1:T(8,128)(2,1)S(1)}, bf16[2,4,128,768]{3,2,0,1:T(8,128)(2,1)S(1)}, u32[]{:S(2)}, u32[]{:S(2)}) collective-permute-start(bf16[2,4,128,768]{3,2,0,1:T(8,128)(2,1)S(1)} %fusion.67), channel_id=1, source_target_pairs={{0,4},{1,3},{2,6},{3,1},{4,0},{5,7},{6,2},{7,5},{8,12},{9,11},{10,... | collective-permute-start | bytes 4718600 | tf_op jit(solution)/shard_map/ppermute | solution.py:47
  490.3 93.4 %collective-permute-start.31 = (bf16[4,128,768]{2,1,0:T(8,128)(2,1)}, bf16[4,128,768]{2,1,0:T(8,128)(2,1)}, u32[]{:S(2)}, u32[]{:S(2)}) collective-permute-start(bf16[4,128,768]{2,1,0:T(8,128)(2,1)} %fusion.70), channel_id=1, source_target_pairs={{0,2},{1,5},{2,0},{3,7},{4,6},{5,1},{6,4},{7,3},{8,10},{9,13},{10,... | collective-permute-start | bytes 2359304 | tf_op jit(solution)/shard_map/ppermute | solution.py:47
  516.5 73.6 %collective-permute-start.22 = (bf16[4,128,768]{2,1,0:T(8,128)(2,1)S(1)}, bf16[4,128,768]{2,1,0:T(8,128)(2,1)}, u32[]{:S(2)}, u32[]{:S(2)}) collective-permute-start(bf16[4,128,768]{2,1,0:T(8,128)(2,1)S(1)} %fusion.69), channel_id=1, source_target_pairs={{0,2},{1,5},{2,0},{3,7},{4,6},{5,1},{6,4},{7,3},{8,10},{9,13},{10,... | collective-permute-start | bytes 2359304 | tf_op jit(solution)/shard_map/ppermute | solution.py:47
  585.5 10.5 %collective-permute-start.32 = (bf16[128,768]{1,0:T(8,128)(2,1)S(1)}, bf16[128,768]{1,0:T(8,128)(2,1)S(1)}, u32[]{:S(2)}, u32[]{:S(2)}) collective-permute-start(bf16[128,768]{1,0:T(8,128)(2,1)S(1)} %get-tuple-element.38), channel_id=1, source_target_pairs={{0,8},{1,9},{2,10},{3,11},{4,12},{5,13},{6,14},{7,15},{8,0},{9,1},... | collective-permute-start | bytes 589832 | tf_op jit(solution)/shard_map/ppermute | solution.py:47
  588.3 11.9 %collective-permute-start.34 = (bf16[128,768]{1,0:T(8,128)(2,1)S(1)}, bf16[128,768]{1,0:T(8,128)(2,1)S(1)}, u32[]{:S(2)}, u32[]{:S(2)}) collective-permute-start(bf16[128,768]{1,0:T(8,128)(2,1)S(1)} %get-tuple-element.39), channel_id=1, source_target_pairs={{0,24},{1,25},{2,26},{3,27},{4,28},{5,29},{6,30},{7,31},{8,16},{9,... | collective-permute-start | bytes 589832 | tf_op jit(solution)/shard_map/ppermute | solution.py:47
  590.1 26.5 %collective-permute-start.33 = (bf16[128,768]{1,0:T(8,128)(2,1)S(1)}, bf16[128,768]{1,0:T(8,128)(2,1)S(1)}, u32[]{:S(2)}, u32[]{:S(2)}) collective-permute-start(bf16[128,768]{1,0:T(8,128)(2,1)S(1)} %get-tuple-element.40), channel_id=1, source_target_pairs={{0,16},{1,17},{2,18},{3,19},{4,20},{5,21},{6,22},{7,23},{8,24},{9,... | collective-permute-start | bytes 589832 | tf_op jit(solution)/shard_map/ppermute | solution.py:47
  591.6 26.8 %collective-permute-start.23 = (bf16[128,768]{1,0:T(8,128)(2,1)S(1)}, bf16[128,768]{1,0:T(8,128)(2,1)S(1)}, u32[]{:S(2)}, u32[]{:S(2)}) collective-permute-start(bf16[128,768]{1,0:T(8,128)(2,1)S(1)} %get-tuple-element.41), channel_id=1, source_target_pairs={{0,8},{1,9},{2,10},{3,11},{4,12},{5,13},{6,14},{7,15},{8,0},{9,1},... | collective-permute-start | bytes 589832 | tf_op jit(solution)/shard_map/ppermute | solution.py:47
  594.2 24.7 %collective-permute-start.25 = (bf16[128,768]{1,0:T(8,128)(2,1)S(1)}, bf16[128,768]{1,0:T(8,128)(2,1)S(1)}, u32[]{:S(2)}, u32[]{:S(2)}) collective-permute-start(bf16[128,768]{1,0:T(8,128)(2,1)S(1)} %get-tuple-element.42), channel_id=1, source_target_pairs={{0,24},{1,25},{2,26},{3,27},{4,28},{5,29},{6,30},{7,31},{8,16},{9,... | collective-permute-start | bytes 589832 | tf_op jit(solution)/shard_map/ppermute | solution.py:47
  596.0 28.6 %collective-permute-start.24 = (bf16[128,768]{1,0:T(8,128)(2,1)S(1)}, bf16[128,768]{1,0:T(8,128)(2,1)S(1)}, u32[]{:S(2)}, u32[]{:S(2)}) collective-permute-start(bf16[128,768]{1,0:T(8,128)(2,1)S(1)} %get-tuple-element.43), channel_id=1, source_target_pairs={{0,16},{1,17},{2,18},{3,19},{4,20},{5,21},{6,22},{7,23},{8,24},{9,... | collective-permute-start | bytes 589832 | tf_op jit(solution)/shard_map/ppermute | solution.py:47
  617.2 9.8 %collective-permute-start.36 = (bf16[128,768]{1,0:T(8,128)(2,1)S(1)}, bf16[128,768]{1,0:T(8,128)(2,1)S(1)}, u32[]{:S(2)}, u32[]{:S(2)}) collective-permute-start(bf16[128,768]{1,0:T(8,128)(2,1)S(1)} %fusion.73), channel_id=1, source_target_pairs={{0,1},{1,0},{2,3},{3,2},{4,5},{5,4},{6,7},{7,6},{8,9},{9,8},{10,11... | collective-permute-start | bytes 589832 | tf_op jit(solution)/shard_map/ppermute | solution.py:47
  618.4 9.8 %collective-permute-start.35 = (bf16[128,768]{1,0:T(8,128)(2,1)S(1)}, bf16[128,768]{1,0:T(8,128)(2,1)S(1)}, u32[]{:S(2)}, u32[]{:S(2)}) collective-permute-start(bf16[128,768]{1,0:T(8,128)(2,1)S(1)} %fusion.73), channel_id=1, source_target_pairs={{0,2},{1,3},{2,0},{3,1},{4,6},{5,7},{6,4},{7,5},{8,10},{9,11},{10,... | collective-permute-start | bytes 589832 | tf_op jit(solution)/shard_map/ppermute | solution.py:47
  624.8 10.0 %collective-permute-start.28 = (bf16[128,768]{1,0:T(8,128)(2,1)S(1)}, bf16[128,768]{1,0:T(8,128)(2,1)}, u32[]{:S(2)}, u32[]{:S(2)}) collective-permute-start(bf16[128,768]{1,0:T(8,128)(2,1)S(1)} %fusion.76), channel_id=1, source_target_pairs={{0,3},{1,2},{2,1},{3,0},{4,7},{5,6},{6,5},{7,4},{8,11},{9,10},{10,... | collective-permute-start | bytes 589832 | tf_op jit(solution)/shard_map/ppermute | solution.py:47
  626.4 10.3 %collective-permute-start.26 = (bf16[128,768]{1,0:T(8,128)(2,1)S(1)}, bf16[128,768]{1,0:T(8,128)(2,1)}, u32[]{:S(2)}, u32[]{:S(2)}) collective-permute-start(bf16[128,768]{1,0:T(8,128)(2,1)S(1)} %fusion.76), channel_id=1, source_target_pairs={{0,2},{1,3},{2,0},{3,1},{4,6},{5,7},{6,4},{7,5},{8,10},{9,11},{10,... | collective-permute-start | bytes 589832 | tf_op jit(solution)/shard_map/ppermute | solution.py:47
  (54 other events, 700.0 us)
Sparse Core Ops, SparseCore 0:
  463.1 116.6 all-reduce.1
where the time goes:
time: 659 us; the launch traced here: 650 us
  local copies, waits for them, and re-layouts  144 us (22%)
  other arithmetic  143 us (22%)
  waiting for transfers between devices  143 us (22%)
  matrix products  119 us (18%)
  blocking collectives  45.8 us (7%)
  starting transfers between devices  40.6 us (6%)
  between operations  15.4 us (2%)
    ppermute x38, waiting for transfers between devices, move(): return lax.ppermute(value, AXES, pairs)  83.7 us
    dot_general x12, matrix products, dot(): return lax.dot_general(a, b, (dims, ((), ())), preferred_element_type=F32)  71.4 us
    psum x1, waiting for transfers between devices, per_device(): smalls = lax.psum(smalls, AXES)  58.8 us
    unnamed x105, local copies, waits for them, and re-layouts  49.5 us
    select_n x12, other arithmetic, flip_if(): return jnp.where(bit == 1, jnp.flip(value, axis), value)  49 us
    all_gather x1, blocking collectives, per_device(): small = lax.all_gather(small, 'batch', axis=1, tiled=True)  45.8 us
    ppermute x38, starting transfers between devices, move(): return lax.ppermute(value, AXES, pairs)  40.5 us
    convert_element_type x2, local copies, waits for them, and re-layouts, per_device(): jnp.stack([g_q, g_k, g_v], axis=2).astype(BF).reshape(-1, 3 * width)  19.5 us
  transfers between devices with their start and end apart: 39, of which 13 were waited for; matrix products, arithmetic and copies ran while one was open for 23% of the time, Pallas kernels for 0%

commit v1 on v0

--- a/solution.py
+++ b/solution.py
@@ -1,3 +1,4 @@
+import functools
 import jax
 import jax.numpy as jnp
 from jax import lax
@@ -8,6 +9,15 @@
 AXES = ("batch", "rep")
 BF = jnp.bfloat16
 F32 = jnp.float32
+
+
+def serve_rails(chunk, group_axis):
+    all_rows = jax.lax.all_gather(chunk, group_axis)
+    found_now = jnp.sum(all_rows, 0)
+    return found_now
+
+
+inputs_return_all = functools.partial(serve_rails, group_axis=AXES)
 
 
 def layer_norm(values, gain, shift):
@@ -184,7 +194,7 @@
         [gg1, gg2, gb1, gb_packed[:width], gb_packed[2 * width :], gb_out, gb2, gb_down, gb_up]
         + [zero] * 7
     )
-    smalls = lax.psum(smalls, AXES)
+    smalls = inputs_return_all(smalls)
     smalls = lax.dynamic_slice_in_dim(
         smalls, lax.axis_index("batch") * (width // nb), width // nb, 1
     )

time: 659 us -> 603 us (0.915)
  waiting for transfers between devices: 143 us -> 90 us
    psum x1 -> x0, waiting for transfers between devices: 58.8 us -> none  [per_device(): smalls = lax.psum(smalls, AXES)]
    unnamed x105 -> x103, local copies, waits for them, and re-layouts: 49.5 us -> 49.4 us
  transfers between devices with their start and end apart: 39 -> 39, of which waited for: 13 -> 13; matrix products, arithmetic and copies ran while one was open for 23% -> 25% of each run, Pallas kernels for 0% -> 0%
where the time goes in v1:
time: 603 us; the launch traced here: 595 us
  other arithmetic  146 us (24%)
  local copies, waits for them, and re-layouts  141 us (23%)
  matrix products  119 us (20%)
  waiting for transfers between devices  90 us (15%)
  blocking collectives  45.8 us (8%)
  starting transfers between devices  37.6 us (6%)
  between operations  15.4 us (3%)
    ppermute x38, waiting for transfers between devices, move(): return lax.ppermute(value, AXES, pairs)  90 us
    dot_general x12, matrix products, dot(): return lax.dot_general(a, b, (dims, ((), ())), preferred_element_type=F32)  71.3 us
    unnamed x103, local copies, waits for them, and re-layouts  49.4 us
    select_n x12, other arithmetic, flip_if(): return jnp.where(bit == 1, jnp.flip(value, axis), value)  49 us
    all_gather x1, blocking collectives, per_device(): small = lax.all_gather(small, 'batch', axis=1, tiled=True)  45.8 us
    ppermute x38, starting transfers between devices, move(): return lax.ppermute(value, AXES, pairs)  37.5 us
    convert_element_type x2, local copies, waits for them, and re-layouts, per_device(): jnp.stack([g_q, g_k, g_v], axis=2).astype(BF).reshape(-1, 3 * width)  19.5 us
    sub x1, other arithmetic, per_device(): raised = jnp.exp(scores - top)  19 us
  transfers between devices with their start and end apart: 39, of which 13 were waited for; matrix products, arithmetic and copies ran while one was open for 25% of the time, Pallas kernels for 0%

profile of v1, /device:TPU:0, one launch (start us, length us, event | category | flops | bytes accessed | tf_op | source)
XLA Modules:
  0.0 594.6 jit_solution(3247819331048956905)
XLA Ops:
  8.3 5.1 collective-permute-start.2
  20.9 45.8 %all_gather.9 = bf16[9,1024]{1,0:T(8,128)(2,1)S(1)} all-gather(bf16[9,128]{1,0:T(8,128)(2,1)S(1)} %pad_maximum_fusion.9), channel_id=1, replica_groups=mesh['batch'=8,'rep'=4] {'batch'}, dimensions={1}, use_global_device_ids=true | all-gather | bytes 20736 | tf_op jit(solution)/shard_map/all_gather | solution.py:140
  77.2 7.4 %collective-permute-done.4 = bf16[4,32,3072]{2,1,0:T(8,128)(2,1)} collective-permute-done((bf16[4,32,3072]{2,1,0:T(8,128)(2,1)}, bf16[4,32,3072]{2,1,0:T(8,128)(2,1)}, u32[]{:S(2)}, u32[]{:S(2)}) %collective-permute-start.4) | collective-permute-done | bytes 786464 | tf_op jit(solution)/shard_map/ppermute | solution.py:57
  89.4 12.0 %collective-permute-done.14 = bf16[4,32,3072]{2,1,0:T(8,128)(2,1)S(1)} collective-permute-done((bf16[4,32,3072]{2,1,0:T(8,128)(2,1)S(1)}, bf16[4,32,3072]{2,1,0:T(8,128)(2,1)S(1)}, u32[]{:S(2)}, u32[]{:S(2)}) %collective-permute-start.14) | collective-permute-done | bytes 786464 | tf_op jit(solution)/shard_map/ppermute | solution.py:57
  107.8 8.4 %collective-permute-done.15 = bf16[4,32,3072]{2,1,0:T(8,128)(2,1)} collective-permute-done((bf16[4,32,3072]{2,1,0:T(8,128)(2,1)S(1)}, bf16[4,32,3072]{2,1,0:T(8,128)(2,1)}, u32[]{:S(2)}, u32[]{:S(2)}) %collective-permute-start.15) | collective-permute-done | bytes 786464 | tf_op jit(solution)/shard_map/ppermute | solution.py:57
  130.7 7.5 %reverse_select_fusion.4 = bf16[2,2,2,4,32,3072]{5,4,3,2,1,0:T(8,128)(2,1)S(1)} fusion(bf16[2,2,2,4,32,3072]{5,4,3,2,1,0:T(8,128)(2,1)} %pad_maximum_fusion.2, pred[]{:T(512)S(6)} %eq.23), kind=kLoop, calls=%fused_computation.14 | loop fusion | flops 3145728 | bytes 12582913 | tf_op jit(solution)/shard_map/jit(_where)/select_n | solution.py:61
  147.1 7.6 %reverse_select_fusion.7 = bf16[2,2,2,4,32,3072]{5,4,2,0,1,3:T(8,128)(2,1)S(1)} fusion(bf16[2,2,2,4,32,3072]{5,4,2,0,1,3:T(8,128)(2,1)} %reverse_select_fusion.8, pred[]{:T(512)S(6)} %eq.21), kind=kLoop, calls=%fused_computation.17 | loop fusion | flops 3145728 | bytes 12582913 | tf_op jit(solution)/shard_map/jit(_where)/select_n | solution.py:61
  169.1 7.5 %reverse_select_fusion.5 = bf16[2,2,2,2,2,32,3072]{6,5,2,0,1,4,3:T(8,128)(2,1)S(1)} fusion(bf16[2,2,2,2,2,32,3072]{6,5,2,0,1,4,3:T(8,128)(2,1)} %reverse_select_fusion.6, pred[]{:T(512)S(6)} %eq.19), kind=kLoop, calls=%fused_computation.15 | loop fusion | flops 3145728 | bytes 12582913 | tf_op jit(solution)/shard_map/jit(_where)/select_n | solution.py:61
  181.3 8.7 %fusion.5 = bf16[128,8,24,128]{3,1,2,0:T(8,128)(2,1)} fusion(f32[3072]{0:T(1024)S(1)} %pad_maximum_fusion.8, bf16[1024,1024]{1,0:T(8,128)(2,1)S(1)} %bitcast.351, bf16[1024,3072]{1,0:T(8,128)(2,1)S(1)} %bitcast.344), kind=kOutput, calls=%fused_computation.22 | convolution fusion | flops 6448742400 | bytes 14692352 | tf_op jit(solution)/shard_map/dot_general | solution.py:149
  202.4 10.4 %fusion.52 = f32[2,8,512,512]{2,3,1,0:T(8,128)} fusion(bf16[2,512,1,8,128]{4,3,2,1,0:T(8,128)(2,1)} %get-tuple-element.42, bf16[2,512,1,8,128]{4,3,2,1,0:T(8,128)(2,1)} %get-tuple-element.40), kind=kOutput, calls=%fused_computation.106 | convolution fusion | flops 1073741824 | bytes 20971520 | tf_op jit(solution)/shard_map/iqhd,ikhd->ihqk/dot_general | solution.py:157
  212.7 19.0 %fusion.100 = (f32[2,8,512]{2,1,0:T(8,128)S(1)}, f32[2,8,512,512]{2,3,1,0:T(8,128)}) fusion(f32[2,8,512,512]{2,3,1,0:T(8,128)} %fusion.52), kind=kOutput, calls=%fused_computation.208 | output fusion | flops 16777728 | bytes 33587200 | tf_op jit(solution)/shard_map/sub | solution.py:159
  231.8 8.4 %convert_bitcast_fusion.2 = bf16[2,512,8,128]{1,3,2,0:T(8,128)(2,1)} fusion(bf16[2,512,1,8,128]{1,4,3,0,2:T(8,128)(2,1)S(1)} %copy-done.21, f32[2,8,512,512]{2,3,1,0:T(8,128)} %get-tuple-element.83, f32[2,8,512]{2,1,0:T(8,128)S(1)} %get-tuple-element.82), kind=kOutput, calls=%fused_computation.105 | convolution fusion | flops 1083179008 | bytes 21004288 | tf_op jit(solution)/shard_map/ihqk,ikhd->iqhd/dot_general | solution.py:162
  252.5 5.9 convert_reduce_fusion.2
  288.0 10.7 %fusion.38 = bf16[2,512,1,8,128]{1,4,3,0,2:T(8,128)(2,1)} fusion(bf16[2,512,8,128]{1,3,2,0:T(8,128)(2,1)} %copy.89, f32[2,8,512,512]{2,3,1,0:T(8,128)} %get-tuple-element.83, f32[2,8,512]{2,1,0:T(8,128)S(1)} %get-tuple-element.82), kind=kOutput, calls=%fused_computation.94 | convolution fusion | flops 1082130432 | bytes 21004288 | tf_op jit(solution)/shard_map/ihqk,iqhd->ikhd/dot_general | solution.py:182
  298.7 10.9 %multiply_reduce_fusion = (f32[2,8,512]{2,1,0:T(8,128)S(1)}, f32[2,8,512,512]{2,3,1,0:T(8,128)}) fusion(f32[2,8,512,512]{2,3,1,0:T(8,128)} %get-tuple-element.83, f32[2,8,512]{2,1,0:T(8,128)S(1)} %get-tuple-element.82, bf16[2,512,8,128]{1,3,2,0:T(8,128)(2,1)S(1)} %copy-done.24, bf16[2,512,1,8,128]{1,4,3,0,2:T(8,128)(2,1)S(1)} %copy-done.22), kind=kOutput, calls=%fused_computation.2 | convolution fusion | flops 1086316544 | bytes 37814272 | tf_op jit(solution)/shard_map/iqhd,ikhd->ihqk/dot_general | solution.py:183
  309.6 11.9 %multiply_convert_fusion = bf16[2,8,512,512]{2,3,1,0:T(8,128)(2,1)S(1)} fusion(f32[2,8,512,512]{2,3,1,0:T(8,128)} %get-tuple-element.88, f32[2,8,512]{2,1,0:T(8,128)S(1)} %get-tuple-element.87, f32[2,8,512,512]{2,3,1,0:T(8,128)} %get-tuple-element.83, f32[2,8,512]{2,1,0:T(8,128)S(1)} %get-tuple-element.82), kind=kLoop, calls=%fused_computation.1 | loop fusion | flops 16777216 | bytes 42008576 | tf_op jit(solution)/shard_map/convert_element_type | solution.py:184
  331.1 5.7 pad_maximum_fusion
  336.8 16.9 %reshape.233 = f32[4,2,128,2,2,768]{2,1,0,5,4,3:T(2,128)} reshape(f32[1024,3072]{0,1:T(8,128)} %pad_maximum_fusion) | data formatting | bytes 25165824 | tf_op jit(solution)/shard_map/reshape | solution.py:94
  353.7 6.6 %constant_dynamic-slice_fusion.1 = bf16[4,2,128,1,2,768]{2,1,0,5,4,3:T(2,128)(2,1)} fusion(f32[4,2,128,2,2,768]{2,1,0,5,4,3:T(2,128)} %reshape.233, s32[]{:T(128)S(6)} %select_n.250), kind=kLoop, calls=%fused_computation.178 | loop fusion | bytes 6291460 | tf_op jit(solution)/shard_map/jit(dynamic_index_in_dim)/dynamic_slice | solution.py:97
  360.3 8.7 %copy.125 = bf16[4,2,128,1,2,768]{5,2,0,1,4,3:T(8,128)(2,1)} copy(bf16[4,2,128,1,2,768]{2,1,0,5,4,3:T(2,128)(2,1)} %constant_dynamic-slice_fusion.1) | data formatting | bytes 6291456
  369.4 6.1 %convert_reduce_fusion = (f32[3,8,128]{2,1,0:T(8,128)S(1)}, bf16[2,512,3,8,128]{1,4,3,0,2:T(8,128)(2,1)}) fusion(bf16[2,512,1,8,128]{1,4,3,0,2:T(8,128)(2,1)} %fusion.38, bf16[2,512,1,8,128]{1,4,3,0,2:T(8,128)(2,1)} %multiply_bitcast_fusion, bf16[2,512,1,8,128]{1,4,3,0,2:T(8,128)(2,1)} %multiply_bitcast_fusion.1), kind=kLoop, calls=%fused_computation.8 | loop fusion | flops 12579840 | bytes 12595200 | tf_op jit(solution)/shard_map/reduce_sum | solution.py:189
  375.5 9.2 %copy.91 = bf16[2,512,3,8,128]{4,3,2,1,0:T(8,128)(2,1)} copy(bf16[2,512,3,8,128]{1,4,3,0,2:T(8,128)(2,1)} %get-tuple-element.37) | data formatting | bytes 12582912 | tf_op jit(solution)/shard_map/convert_element_type | solution.py:187
  384.6 10.3 %convert_element_type.247 = bf16[1024,3072]{1,0:T(8,128)(2,1)} reshape(bf16[2,512,3,8,128]{4,3,2,1,0:T(8,128)(2,1)} %copy.91) | data formatting | bytes 12582912 | tf_op jit(solution)/shard_map/convert_element_type | solution.py:187
  394.9 12.3 %fusion.93 = (f32[1024]{0:T(1024)S(1)}, f32[1024]{0:T(1024)S(1)}, f32[1024,1024]{1,0:T(8,128)}) fusion(f32[1024]{0:T(1024)S(1)} %bitcast.373, f32[1024]{0:T(1024)S(1)} %bitcast.378, bf16[1,2,512,1024]{3,2,1,0:T(8,128)(2,1)S(1)} %copy-done.2, bf16[1024,3072]{1,0:T(8,128)(2,1)} %convert_element_type.247, bf16[1024,3072]{1,0:T(8,128)(2,1)} %bitcast.345), kind=kOutput, calls=%fused_computation.202 | convolution fusion | flops 6448740352 | bytes 18890752 | tf_op jit(solution)/shard_map/dot_general | solution.py:149
  407.3 8.9 %copy.92 = bf16[3072,1024]{1,0:T(8,128)(2,1)} copy(bf16[3072,1024]{0,1:T(8,128)(2,1)} %bitcast.326) | data formatting | bytes 12582912 | tf_op jit(solution)/shard_map/dot_general | solution.py:149
  416.2 5.1 fusion.25
  425.3 9.5 %fusion.102 = f32[4,2,128,2,2,768]{5,2,4,3,1,0:T(8,128)S(1)} fusion(bf16[4,2,128,1024,1,1]{3,2,5,4,1,0:T(8,128)(2,1)} %bitcast.354, bf16[2,2,768,1024,1,1]{3,2,1,0,5,4:T(8,128)(2,1)} %bitcast.346), kind=kOutput, calls=%fused_computation.210 | convolution fusion | flops 6442450944 | bytes 20971520 | tf_op jit(solution)/shard_map/dot_general | solution.py:149
  443.5 7.6 %constant_dynamic-slice_fusion.2 = f32[4,2,128,1,2,768]{2,1,0,5,4,3:T(2,128)} fusion(f32[4,2,128,2,2,768]{2,1,0,5,4,3:T(2,128)} %reshape.233, s32[]{:T(128)S(6)} %select_n.249), kind=kLoop, calls=%fused_computation.179 | loop fusion | bytes 12582916 | tf_op jit(solution)/shard_map/dynamic-slice.2
  451.1 10.5 %copy.124 = f32[4,2,128,1,2,768]{5,2,0,1,4,3:T(8,128)} copy(f32[4,2,128,1,2,768]{2,1,0,5,4,3:T(2,128)} %constant_dynamic-slice_fusion.2) | data formatting | bytes 12582912
  480.6 8.4 %add_convert_fusion.2 = bf16[1024,1024]{1,0:T(8,128)(2,1)} fusion(f32[1024,1024]{1,0:T(8,128)} %copy-done.10, f32[1024]{0:T(1024)S(1)} %bitcast.396, bf16[1024,3072]{1,0:T(8,128)(2,1)} %bitcast.337, f32[1024,1024]{1,0:T(8,128)} %copy-done.41, f32[1024]{0:T(1024)S(1)} %bitcast.395), kind=kOutput, calls=%fused_computation.75 | convolution fusion | flops 2161115136 | bytes 12591104 | tf_op jit(solution)/shard_map/dot_general | solution.py:149
  491.7 28.2 %collective-permute-done.21 = bf16[2,4,128,768]{3,2,0,1:T(8,128)(2,1)S(1)} collective-permute-done((bf16[2,4,128,768]{3,2,0,1:T(8,128)(2,1)S(1)}, bf16[2,4,128,768]{3,2,0,1:T(8,128)(2,1)S(1)}, u32[]{:S(2)}, u32[]{:S(2)}) %collective-permute-start.21) | collective-permute-done | bytes 1572896 | tf_op jit(solution)/shard_map/ppermute | solution.py:57
  544.2 17.5 %collective-permute-done.33 = bf16[128,768]{1,0:T(8,128)(2,1)S(1)} collective-permute-done((bf16[128,768]{1,0:T(8,128)(2,1)S(1)}, bf16[128,768]{1,0:T(8,128)(2,1)S(1)}, u32[]{:S(2)}, u32[]{:S(2)}) %collective-permute-start.33) | collective-permute-done | bytes 196640 | tf_op jit(solution)/shard_map/ppermute | solution.py:57
  (278 shorter events, 220.6 us)
Async XLA Ops:
  7.2 519.2 %all-gather.3.cloned.1.call-start = ((), (), s32[]{:S(2)}) async-start(), calls=%async_computation | async-start | bytes 2162688 | tf_op jit(solution)/shard_map/all_gather | solution.py:15
  8.3 59.0 %collective-permute-start.2 = (bf16[32,3072]{1,0:T(8,128)(2,1)S(1)}, bf16[32,3072]{1,0:T(8,128)(2,1)S(1)}, u32[]{:S(2)}, u32[]{:S(2)}) collective-permute-start(bf16[32,3072]{1,0:T(8,128)(2,1)S(1)} %fusion.119), channel_id=1, source_target_pairs={{0,24},{1,25},{2,26},{3,27},{4,28},{5,29},{6,30},{7,31},{8,16},{9,... | collective-permute-start | bytes 589832 | tf_op jit(solution)/shard_map/ppermute | solution.py:57
  13.4 54.2 %collective-permute-start.1 = (bf16[32,3072]{1,0:T(8,128)(2,1)S(1)}, bf16[32,3072]{1,0:T(8,128)(2,1)S(1)}, u32[]{:S(2)}, u32[]{:S(2)}) collective-permute-start(bf16[32,3072]{1,0:T(8,128)(2,1)S(1)} %fusion.119), channel_id=1, source_target_pairs={{0,16},{1,17},{2,18},{3,19},{4,20},{5,21},{6,22},{7,23},{8,24},{9,... | collective-permute-start | bytes 589832 | tf_op jit(solution)/shard_map/ppermute | solution.py:57
  13.5 54.2 %collective-permute-start = (bf16[32,3072]{1,0:T(8,128)(2,1)S(1)}, bf16[32,3072]{1,0:T(8,128)(2,1)S(1)}, u32[]{:S(2)}, u32[]{:S(2)}) collective-permute-start(bf16[32,3072]{1,0:T(8,128)(2,1)S(1)} %fusion.119), channel_id=1, source_target_pairs={{0,8},{1,9},{2,10},{3,11},{4,12},{5,13},{6,14},{7,15},{8,0},{9,1},... | collective-permute-start | bytes 589832 | tf_op jit(solution)/shard_map/ppermute | solution.py:57
  16.0 57.5 %collective-permute-start.12 = (bf16[32,3072]{1,0:T(8,128)(2,1)}, bf16[32,3072]{1,0:T(8,128)(2,1)S(1)}, u32[]{:S(2)}, u32[]{:S(2)}) collective-permute-start(bf16[32,3072]{1,0:T(8,128)(2,1)} %fusion.120), channel_id=1, source_target_pairs={{0,24},{1,25},{2,26},{3,27},{4,28},{5,29},{6,30},{7,31},{8,16},{9,... | collective-permute-start | bytes 589832 | tf_op jit(solution)/shard_map/ppermute | solution.py:57
  19.7 53.9 %collective-permute-start.11 = (bf16[32,3072]{1,0:T(8,128)(2,1)}, bf16[32,3072]{1,0:T(8,128)(2,1)S(1)}, u32[]{:S(2)}, u32[]{:S(2)}) collective-permute-start(bf16[32,3072]{1,0:T(8,128)(2,1)} %fusion.120), channel_id=1, source_target_pairs={{0,16},{1,17},{2,18},{3,19},{4,20},{5,21},{6,22},{7,23},{8,24},{9,... | collective-permute-start | bytes 589832 | tf_op jit(solution)/shard_map/ppermute | solution.py:57
  68.6 16.0 %collective-permute-start.4 = (bf16[4,32,3072]{2,1,0:T(8,128)(2,1)}, bf16[4,32,3072]{2,1,0:T(8,128)(2,1)}, u32[]{:S(2)}, u32[]{:S(2)}) collective-permute-start(bf16[4,32,3072]{2,1,0:T(8,128)(2,1)} %get-tuple-element.62), channel_id=1, source_target_pairs={{0,2},{1,5},{2,0},{3,7},{4,6},{5,1},{6,4},{7,3},{8,10},{9,13},{10,... | collective-permute-start | bytes 2359304 | tf_op jit(solution)/shard_map/ppermute | solution.py:57
  70.1 17.6 %collective-permute-start.3 = (bf16[4,32,3072]{2,1,0:T(8,128)(2,1)}, bf16[4,32,3072]{2,1,0:T(8,128)(2,1)}, u32[]{:S(2)}, u32[]{:S(2)}) collective-permute-start(bf16[4,32,3072]{2,1,0:T(8,128)(2,1)} %get-tuple-element.62), channel_id=1, source_target_pairs={{0,4},{1,3},{2,6},{3,1},{4,0},{5,7},{6,2},{7,5},{8,12},{9,11},{10,... | collective-permute-start | bytes 2359304 | tf_op jit(solution)/shard_map/ppermute | solution.py:57
  73.5 48.8 %collective-permute-start.6 = (bf16[4,32,3072]{2,1,0:T(8,128)(2,1)}, bf16[4,32,3072]{2,1,0:T(8,128)(2,1)S(1)}, u32[]{:S(2)}, u32[]{:S(2)}) collective-permute-start(bf16[4,32,3072]{2,1,0:T(8,128)(2,1)} %get-tuple-element.62), channel_id=1, source_target_pairs={{0,1},{1,0},{2,3},{3,2},{4,5},{5,4},{6,7},{7,6},{8,9},{9,8},{10,11... | collective-permute-start | bytes 2359304 | tf_op jit(solution)/shard_map/ppermute | solution.py:57
  74.7 26.7 %collective-permute-start.14 = (bf16[4,32,3072]{2,1,0:T(8,128)(2,1)S(1)}, bf16[4,32,3072]{2,1,0:T(8,128)(2,1)S(1)}, u32[]{:S(2)}, u32[]{:S(2)}) collective-permute-start(bf16[4,32,3072]{2,1,0:T(8,128)(2,1)S(1)} %get-tuple-element.64), channel_id=1, source_target_pairs={{0,2},{1,5},{2,0},{3,7},{4,6},{5,1},{6,4},{7,3},{8,10},{9,13},{10,... | collective-permute-start | bytes 2359304 | tf_op jit(solution)/shard_map/ppermute | solution.py:57
  76.0 25.4 %collective-permute-start.13 = (bf16[4,32,3072]{2,1,0:T(8,128)(2,1)S(1)}, bf16[4,32,3072]{2,1,0:T(8,128)(2,1)S(1)}, u32[]{:S(2)}, u32[]{:S(2)}) collective-permute-start(bf16[4,32,3072]{2,1,0:T(8,128)(2,1)S(1)} %get-tuple-element.64), channel_id=1, source_target_pairs={{0,4},{1,3},{2,6},{3,1},{4,0},{5,7},{6,2},{7,5},{8,12},{9,11},{10,... | collective-permute-start | bytes 2359304 | tf_op jit(solution)/shard_map/ppermute | solution.py:57
  84.6 23.0 %collective-permute-start.5 = (bf16[4,32,3072]{2,1,0:T(8,128)(2,1)}, bf16[4,32,3072]{2,1,0:T(8,128)(2,1)S(1)}, u32[]{:S(2)}, u32[]{:S(2)}) collective-permute-start(bf16[4,32,3072]{2,1,0:T(8,128)(2,1)} %collective-permute-done.4), channel_id=1, source_target_pairs={{0,4},{1,3},{2,6},{3,1},{4,0},{5,7},{6,2},{7,5},{8,12},{9,11},{10,... | collective-permute-start | bytes 2359304 | tf_op jit(solution)/shard_map/ppermute | solution.py:57
  87.7 29.7 %collective-permute-start.8 = (bf16[4,32,3072]{2,1,0:T(8,128)(2,1)}, bf16[4,32,3072]{2,1,0:T(8,128)(2,1)S(1)}, u32[]{:S(2)}, u32[]{:S(2)}) collective-permute-start(bf16[4,32,3072]{2,1,0:T(8,128)(2,1)} %collective-permute-done.4), channel_id=1, source_target_pairs={{0,1},{1,0},{2,3},{3,2},{4,5},{5,4},{6,7},{7,6},{8,9},{9,8},{10,11... | collective-permute-start | bytes 2359304 | tf_op jit(solution)/shard_map/ppermute | solution.py:57
  101.4 16.6 %collective-permute-start.7 = (bf16[4,32,3072]{2,1,0:T(8,128)(2,1)}, bf16[4,32,3072]{2,1,0:T(8,128)(2,1)S(1)}, u32[]{:S(2)}, u32[]{:S(2)}) collective-permute-start(bf16[4,32,3072]{2,1,0:T(8,128)(2,1)} %collective-permute-done.3), channel_id=1, source_target_pairs={{0,1},{1,0},{2,3},{3,2},{4,5},{5,4},{6,7},{7,6},{8,9},{9,8},{10,11... | collective-permute-start | bytes 2359304 | tf_op jit(solution)/shard_map/ppermute | solution.py:57
  101.4 14.8 %collective-permute-start.15 = (bf16[4,32,3072]{2,1,0:T(8,128)(2,1)S(1)}, bf16[4,32,3072]{2,1,0:T(8,128)(2,1)}, u32[]{:S(2)}, u32[]{:S(2)}) collective-permute-start(bf16[4,32,3072]{2,1,0:T(8,128)(2,1)S(1)} %collective-permute-done.14), channel_id=1, source_target_pairs={{0,4},{1,3},{2,6},{3,1},{4,0},{5,7},{6,2},{7,5},{8,12},{9,11},{10,... | collective-permute-start | bytes 2359304 | tf_op jit(solution)/shard_map/ppermute | solution.py:57
  107.6 10.6 %collective-permute-start.18 = (bf16[4,32,3072]{2,1,0:T(8,128)(2,1)S(1)}, bf16[4,32,3072]{2,1,0:T(8,128)(2,1)S(1)}, u32[]{:S(2)}, u32[]{:S(2)}) collective-permute-start(bf16[4,32,3072]{2,1,0:T(8,128)(2,1)S(1)} %collective-permute-done.14), channel_id=1, source_target_pairs={{0,1},{1,0},{2,3},{3,2},{4,5},{5,4},{6,7},{7,6},{8,9},{9,8},{10,11... | collective-permute-start | bytes 2359304 | tf_op jit(solution)/shard_map/ppermute | solution.py:57
  369.0 94.0 %collective-permute-start.29 = (bf16[2,2,4,128,768]{4,3,2,0,1:T(8,128)(2,1)}, bf16[2,2,4,128,768]{4,3,2,0,1:T(8,128)(2,1)}, u32[]{:S(2)}, u32[]{:S(2)}) collective-permute-start(bf16[2,2,4,128,768]{4,3,2,0,1:T(8,128)(2,1)} %bitcast.349), channel_id=1, source_target_pairs={{0,1},{1,0},{2,3},{3,2},{4,5},{5,4},{6,7},{7,6},{8,9},{9,8},{10,11... | collective-permute-start | bytes 9437192 | tf_op jit(solution)/shard_map/ppermute | solution.py:57
  441.4 28.0 %collective-permute-start.20 = (bf16[2,2,4,128,768]{4,3,1,0,2:T(8,128)(2,1)}, bf16[2,2,4,128,768]{4,3,1,0,2:T(8,128)(2,1)}, u32[]{:S(2)}, u32[]{:S(2)}) collective-permute-start(bf16[2,2,4,128,768]{4,3,1,0,2:T(8,128)(2,1)} %fusion.36), channel_id=1, source_target_pairs={{0,1},{1,0},{2,3},{3,2},{4,5},{5,4},{6,7},{7,6},{8,9},{9,8},{10,11... | collective-permute-start | bytes 9437192 | tf_op jit(solution)/shard_map/ppermute | solution.py:57
  468.2 21.0 %collective-permute-start.30 = (bf16[2,4,128,768]{3,2,1,0:T(8,128)(2,1)S(1)}, bf16[2,4,128,768]{3,2,1,0:T(8,128)(2,1)S(1)}, u32[]{:S(2)}, u32[]{:S(2)}) collective-permute-start(bf16[2,4,128,768]{3,2,1,0:T(8,128)(2,1)S(1)} %fusion.68), channel_id=1, source_target_pairs={{0,4},{1,3},{2,6},{3,1},{4,0},{5,7},{6,2},{7,5},{8,12},{9,11},{10,... | collective-permute-start | bytes 4718600 | tf_op jit(solution)/shard_map/ppermute | solution.py:57
  479.6 40.4 %collective-permute-start.21 = (bf16[2,4,128,768]{3,2,0,1:T(8,128)(2,1)S(1)}, bf16[2,4,128,768]{3,2,0,1:T(8,128)(2,1)S(1)}, u32[]{:S(2)}, u32[]{:S(2)}) collective-permute-start(bf16[2,4,128,768]{3,2,0,1:T(8,128)(2,1)S(1)} %fusion.67), channel_id=1, source_target_pairs={{0,4},{1,3},{2,6},{3,1},{4,0},{5,7},{6,2},{7,5},{8,12},{9,11},{10,... | collective-permute-start | bytes 4718600 | tf_op jit(solution)/shard_map/ppermute | solution.py:57
  490.6 39.3 %collective-permute-start.31 = (bf16[4,128,768]{2,1,0:T(8,128)(2,1)}, bf16[4,128,768]{2,1,0:T(8,128)(2,1)}, u32[]{:S(2)}, u32[]{:S(2)}) collective-permute-start(bf16[4,128,768]{2,1,0:T(8,128)(2,1)} %fusion.70), channel_id=1, source_target_pairs={{0,2},{1,5},{2,0},{3,7},{4,6},{5,1},{6,4},{7,3},{8,10},{9,13},{10,... | collective-permute-start | bytes 2359304 | tf_op jit(solution)/shard_map/ppermute | solution.py:57
  522.0 13.3 %collective-permute-start.22 = (bf16[4,128,768]{2,1,0:T(8,128)(2,1)S(1)}, bf16[4,128,768]{2,1,0:T(8,128)(2,1)}, u32[]{:S(2)}, u32[]{:S(2)}) collective-permute-start(bf16[4,128,768]{2,1,0:T(8,128)(2,1)S(1)} %fusion.69), channel_id=1, source_target_pairs={{0,2},{1,5},{2,0},{3,7},{4,6},{5,1},{6,4},{7,3},{8,10},{9,13},{10,... | collective-permute-start | bytes 2359304 | tf_op jit(solution)/shard_map/ppermute | solution.py:57
  531.8 12.4 %collective-permute-start.32 = (bf16[128,768]{1,0:T(8,128)(2,1)S(1)}, bf16[128,768]{1,0:T(8,128)(2,1)S(1)}, u32[]{:S(2)}, u32[]{:S(2)}) collective-permute-start(bf16[128,768]{1,0:T(8,128)(2,1)S(1)} %get-tuple-element.47), channel_id=1, source_target_pairs={{0,8},{1,9},{2,10},{3,11},{4,12},{5,13},{6,14},{7,15},{8,0},{9,1},... | collective-permute-start | bytes 589832 | tf_op jit(solution)/shard_map/ppermute | solution.py:57
  533.5 10.6 %collective-permute-start.34 = (bf16[128,768]{1,0:T(8,128)(2,1)S(1)}, bf16[128,768]{1,0:T(8,128)(2,1)S(1)}, u32[]{:S(2)}, u32[]{:S(2)}) collective-permute-start(bf16[128,768]{1,0:T(8,128)(2,1)S(1)} %get-tuple-element.48), channel_id=1, source_target_pairs={{0,24},{1,25},{2,26},{3,27},{4,28},{5,29},{6,30},{7,31},{8,16},{9,... | collective-permute-start | bytes 589832 | tf_op jit(solution)/shard_map/ppermute | solution.py:57
  533.6 28.0 %collective-permute-start.33 = (bf16[128,768]{1,0:T(8,128)(2,1)S(1)}, bf16[128,768]{1,0:T(8,128)(2,1)S(1)}, u32[]{:S(2)}, u32[]{:S(2)}) collective-permute-start(bf16[128,768]{1,0:T(8,128)(2,1)S(1)} %get-tuple-element.49), channel_id=1, source_target_pairs={{0,16},{1,17},{2,18},{3,19},{4,20},{5,21},{6,22},{7,23},{8,24},{9,... | collective-permute-start | bytes 589832 | tf_op jit(solution)/shard_map/ppermute | solution.py:57
  537.2 25.9 %collective-permute-start.23 = (bf16[128,768]{1,0:T(8,128)(2,1)S(1)}, bf16[128,768]{1,0:T(8,128)(2,1)S(1)}, u32[]{:S(2)}, u32[]{:S(2)}) collective-permute-start(bf16[128,768]{1,0:T(8,128)(2,1)S(1)} %get-tuple-element.50), channel_id=1, source_target_pairs={{0,8},{1,9},{2,10},{3,11},{4,12},{5,13},{6,14},{7,15},{8,0},{9,1},... | collective-permute-start | bytes 589832 | tf_op jit(solution)/shard_map/ppermute | solution.py:57
  539.9 24.1 %collective-permute-start.25 = (bf16[128,768]{1,0:T(8,128)(2,1)S(1)}, bf16[128,768]{1,0:T(8,128)(2,1)S(1)}, u32[]{:S(2)}, u32[]{:S(2)}) collective-permute-start(bf16[128,768]{1,0:T(8,128)(2,1)S(1)} %get-tuple-element.51), channel_id=1, source_target_pairs={{0,24},{1,25},{2,26},{3,27},{4,28},{5,29},{6,30},{7,31},{8,16},{9,... | collective-permute-start | bytes 589832 | tf_op jit(solution)/shard_map/ppermute | solution.py:57
  544.2 23.3 %collective-permute-start.24 = (bf16[128,768]{1,0:T(8,128)(2,1)S(1)}, bf16[128,768]{1,0:T(8,128)(2,1)S(1)}, u32[]{:S(2)}, u32[]{:S(2)}) collective-permute-start(bf16[128,768]{1,0:T(8,128)(2,1)S(1)} %get-tuple-element.52), channel_id=1, source_target_pairs={{0,16},{1,17},{2,18},{3,19},{4,20},{5,21},{6,22},{7,23},{8,24},{9,... | collective-permute-start | bytes 589832 | tf_op jit(solution)/shard_map/ppermute | solution.py:57
  563.1 9.6 %collective-permute-start.35 = (bf16[128,768]{1,0:T(8,128)(2,1)S(1)}, bf16[128,768]{1,0:T(8,128)(2,1)S(1)}, u32[]{:S(2)}, u32[]{:S(2)}) collective-permute-start(bf16[128,768]{1,0:T(8,128)(2,1)S(1)} %fusion.73), channel_id=1, source_target_pairs={{0,2},{1,3},{2,0},{3,1},{4,6},{5,7},{6,4},{7,5},{8,10},{9,11},{10,... | collective-permute-start | bytes 589832 | tf_op jit(solution)/shard_map/ppermute | solution.py:57
  567.5 11.7 %collective-permute-start.28 = (bf16[128,768]{1,0:T(8,128)(2,1)S(1)}, bf16[128,768]{1,0:T(8,128)(2,1)}, u32[]{:S(2)}, u32[]{:S(2)}) collective-permute-start(bf16[128,768]{1,0:T(8,128)(2,1)S(1)} %fusion.76), channel_id=1, source_target_pairs={{0,3},{1,2},{2,1},{3,0},{4,7},{5,6},{6,5},{7,4},{8,11},{9,10},{10,... | collective-permute-start | bytes 589832 | tf_op jit(solution)/shard_map/ppermute | solution.py:57
  567.6 11.7 %collective-permute-start.27 = (bf16[128,768]{1,0:T(8,128)(2,1)S(1)}, bf16[128,768]{1,0:T(8,128)(2,1)}, u32[]{:S(2)}, u32[]{:S(2)}) collective-permute-start(bf16[128,768]{1,0:T(8,128)(2,1)S(1)} %fusion.76), channel_id=1, source_target_pairs={{0,1},{1,0},{2,3},{3,2},{4,5},{5,4},{6,7},{7,6},{8,9},{9,8},{10,11... | collective-permute-start | bytes 589832 | tf_op jit(solution)/shard_map/ppermute | solution.py:57
  569.3 12.0 %collective-permute-start.26 = (bf16[128,768]{1,0:T(8,128)(2,1)S(1)}, bf16[128,768]{1,0:T(8,128)(2,1)}, u32[]{:S(2)}, u32[]{:S(2)}) collective-permute-start(bf16[128,768]{1,0:T(8,128)(2,1)S(1)} %fusion.76), channel_id=1, source_target_pairs={{0,2},{1,3},{2,0},{3,1},{4,6},{5,7},{6,4},{7,5},{8,10},{9,11},{10,... | collective-permute-start | bytes 589832 | tf_op jit(solution)/shard_map/ppermute | solution.py:57
  (53 other events, 718.7 us)
Sparse Core Ops, SparseCore 0:
  463.1 58.3 all-gather.2
